TPU v7x, 32 devices: a whole 2x2x4 slice. The times are simulated.
32 devices in a mesh: gx: 4 (over y, x), gy: 4 (over z), gz: 2 (over core).
Axes of the slice: x: 2, y: 2, z: 4, core: 2. Of those that a mesh axis runs over, the one named last changes fastest.
Arguments:
- metric: float32 [6, 64, 128, 256], P(None, 'gx', 'gy', 'gz'), may hold values from -0.9 to 3, as said below
- mass: float32 [64, 128, 256], P('gx', 'gy', 'gz'), may hold values from 0.5 to 2
- shift: float32 [1], replicated, may hold values from 20 to 80
- loads: float32 [4, 64, 128, 256], P(None, 'gx', 'gy', 'gz'), may hold values from -16 to 16
- inputs: float32 [4, 64, 128, 256], P(None, 'gx', 'gy', 'gz'), may hold values from -0.2762136 to 0.2762136
Outputs:
- residual_factor: float32 [4, 64, 128, 256], P(None, 'gx', 'gy', 'gz')
- feedback: float32 [4, 64, 128, 256], P(None, 'gx', 'gy', 'gz')
Inputs may be any that keep to these rules, and one draw needn't show every extreme that they name: `metric`: each node's six factors form a symmetric positive definite matrix: diagonal entries between 0.3 and 3, off-diagonal entries at most 0.3 times the geometric mean of their two diagonal entries in magnitude.
All inputs are finite; a program needn't handle non-finite values.
Results may differ from a plain program's by a relative error of at most 0.00029.
Values sent between devices are 32-bit elements; how exact they have to be, the bound alone decides.
A program may use at most 128 MiB of HBM per device.

v0:
```python
import jax
import jax.numpy as jnp
import numpy as np
from jax import lax
from jax.sharding import PartitionSpec as P

STEPS = 5


gll_points = (
    -1.0,
    -0.8717401485096066,
    -0.5917001814331423,
    -0.2092992179024789,
    0.2092992179024789,
    0.5917001814331423,
    0.8717401485096066,
    1.0,
)
gll_ends = (-14.0, 0.0, 0.0, 0.0, 0.0, 0.0, 0.0, 14.0)


def padded_2(block, sides, width):
    for axis, dim in sides:
        count = lax.axis_size(axis)
        forward = [(i, i + 1) for i in range(count - 1)]
        backward = [(target, source) for source, target in forward]
        low = lax.ppermute(
            lax.slice_in_dim(block, block.shape[dim] - width, None, axis=dim), axis, forward
        )
        high = lax.ppermute(lax.slice_in_dim(block, 0, width, axis=dim), axis, backward)
        block = jnp.concatenate([low, block, high], axis=dim)
    return block


def gll_table():
    points = np.array(gll_points)
    values = (429.0 * points**7 - 693.0 * points**5 + 315.0 * points**3 - 35.0 * points) / 16.0
    table = np.zeros((8, 8))
    for row in range(8):
        for column in range(8):
            if row != column:
                table[row, column] = values[row] / (values[column] * (points[row] - points[column]))
    table[0, 0] = -14.0
    table[7, 7] = 14.0
    return table


def derive_first(field, matrix):
    count, width, height, depth = field.shape
    shaped = field.reshape(count, width // 8, 8, height, depth)
    return jnp.einsum("ma,ceayz->cemyz", matrix, shaped, precision=lax.Precision.HIGHEST).reshape(
        field.shape
    )


def derive_second(field, matrix):
    count, width, height, depth = field.shape
    shaped = field.reshape(count, width, height // 8, 8, depth)
    return jnp.einsum("mb,cxebz->cxemz", matrix, shaped, precision=lax.Precision.HIGHEST).reshape(
        field.shape
    )


def derive_third(field, block):
    return jnp.einsum("cxyk,mk->cxym", field, block, precision=lax.Precision.HIGHEST)


def pair_fold(padded, dim):
    length = padded.shape[dim] - 2
    phase = jnp.arange(length) % 8
    shape = [1] * padded.ndim
    shape[dim] = length
    upper = (phase == 7).reshape(shape)
    lower = (phase == 0).reshape(shape)
    middle = lax.slice_in_dim(padded, 1, length + 1, axis=dim)
    after = lax.slice_in_dim(padded, 2, length + 2, axis=dim)
    before = lax.slice_in_dim(padded, 0, length, axis=dim)
    return middle + jnp.where(upper, after, 0.0) + jnp.where(lower, before, 0.0)


def assemble(field):
    padded = padded_2(field, (("gx", 1), ("gy", 2), ("gz", 3)), 1)
    return pair_fold(pair_fold(pair_fold(padded, 1), 2), 3)


def local_apply(field, metric, scaled_mass, table, block):
    slope_first = derive_first(field, table)
    slope_second = derive_second(field, table)
    slope_third = derive_third(field, block)
    flux_first = metric[0] * slope_first + metric[3] * slope_second + metric[4] * slope_third
    flux_second = metric[3] * slope_first + metric[1] * slope_second + metric[5] * slope_third
    flux_third = metric[4] * slope_first + metric[5] * slope_second + metric[2] * slope_third
    result = derive_first(flux_first, table.T) + derive_second(flux_second, table.T)
    return result + derive_third(flux_third, block.T) + scaled_mass * field


def local(metric, mass, shift, loads, inputs):
    table_np = gll_table()
    columns, width, height, depth = loads.shape
    table = jnp.asarray(table_np, jnp.float32)
    squares = table * table
    block = jnp.asarray(np.kron(np.eye(depth // 8), table_np), jnp.float32)
    block_squares = jnp.asarray(np.kron(np.eye(depth // 8), table_np * table_np), jnp.float32)
    ends_np = np.array(gll_ends)
    ends_first = jnp.asarray(np.tile(ends_np, width // 8), jnp.float32)[:, None, None]
    ends_second = jnp.asarray(np.tile(ends_np, height // 8), jnp.float32)[None, :, None]
    ends_third = jnp.asarray(np.tile(ends_np, depth // 8), jnp.float32)[None, None, :]
    scale = shift[0]
    scaled_mass = scale * mass
    jdiag = derive_first(metric[0:1], squares.T) + derive_second(metric[1:2], squares.T)
    jdiag = jdiag + derive_third(metric[2:3], block_squares.T)
    cross = (
        ends_first * ends_second * metric[3]
        + ends_first * ends_third * metric[4]
        + ends_second * ends_third * metric[5]
    )
    jdiag = jdiag + (2.0 * cross + scaled_mass)[None]
    stacked = jnp.concatenate(
        [jnp.ones((1, width, height, depth), jnp.float32), jdiag, mass[None], loads, inputs], 0
    )
    assembled = assemble(stacked)
    weight = 1.0 / assembled[0]
    precond = 1.0 / assembled[1]
    mtotal = assembled[2]
    rhs = assembled[3 : 3 + columns]
    drive = assembled[3 + columns :]

    def products(first, second):
        return jnp.sum(first * second * weight, axis=(1, 2, 3))

    def spread(values):
        return values[:, None, None, None]

    solution = jnp.zeros_like(rhs)

    def residual_energy(residual, smooth):
        return lax.psum(products(residual, smooth), ("gx", "gy", "gz"))

    residual = rhs
    smooth = precond * residual
    direction = smooth
    energy = residual_energy(residual, smooth)
    for step in range(STEPS):
        image = assemble(local_apply(direction, metric, scaled_mass, table, block))
        alpha = energy / lax.psum(products(direction, image), ("gx", "gy", "gz"))
        solution = solution + spread(alpha) * direction
        if step + 1 < STEPS:
            residual = residual - spread(alpha) * image
            smooth = precond * residual
            fresh = residual_energy(residual, smooth)
            direction = smooth + spread(fresh / energy) * direction
            energy = fresh
    local_coupling = jnp.einsum(
        "cxyz,jxyz->cj", solution * weight, drive, precision=lax.Precision.HIGHEST
    )
    coupling = lax.psum(local_coupling, ("gx", "gy", "gz"))
    identity = jnp.eye(columns, dtype=jnp.float32)
    ymat = identity + jnp.dot(coupling, coupling.T, precision=lax.Precision.HIGHEST)
    factor = jnp.linalg.cholesky(ymat)
    inverse = jax.scipy.linalg.cho_solve((factor, True), identity)
    gain_coef = jax.scipy.linalg.cho_solve((factor, True), coupling)
    heat = mtotal * solution
    twice = 2.0 * scale
    residual_factor = rhs - twice * jnp.einsum(
        "cxyz,cj->jxyz", heat, inverse, precision=lax.Precision.HIGHEST
    )
    feedback = twice * jnp.einsum("cxyz,cj->jxyz", heat, gain_coef, precision=lax.Precision.HIGHEST)
    return (residual_factor, feedback)


def solution(mesh):
    return jax.shard_map(
        local,
        mesh=mesh,
        in_specs=(
            P(None, "gx", "gy", "gz"),
            P("gx", "gy", "gz"),
            P(),
            P(None, "gx", "gy", "gz"),
            P(None, "gx", "gy", "gz"),
        ),
        out_specs=(P(None, "gx", "gy", "gz"), P(None, "gx", "gy", "gz")),
        check_vma=False,
    )
```

profile of v0, /device:TPU:14, one launch (start us, length us, event | category | flops | bytes accessed | tf_op | source)
XLA Modules:
  0.0 764.7 jit_solution(6969534985200165755)
XLA Ops:
  11.3 4.6 collective-permute-start.1
  15.9 3.1 collective-permute-done
  19.5 3.5 collective-permute-start.2
  23.0 2.4 collective-permute-start.3
  26.1 3.5 collective-permute-done.3
  30.2 4.5 fusion.188
  34.7 3.2 copy.93
  39.2 3.2 copy.94
  43.7 3.0 copy.95
  46.7 3.1 copy.96
  49.7 10.5 %pad_maximum_fusion = f32[11,18,34,130]{3,2,1,0:T(8,128)S(1)} fusion(f32[11,18,34,1]{3,2,1,0:T(8,128)} %copy.96, f32[11,18,1,128]{3,2,1,0:T(1,128)S(1)} %collective-permute-done.3, f32[11,1,32,128]{3,2,1,0:T(8,128)S(1)} %collective-permute-done.1, f32[11,16,32,128]{3,2,1,0:T(8,128)} %copy-done.16, f32[11,1,32,128]{3,2,1,0:T(8,128)S(1)} %collective-permute-done, ...), kind=kLoop, calls=%fused_computation | loop fusion | flops 5250960 | bytes 7001280 | tf_op jit(solution)/shard_map/concatenate | solution.py:32
  76.9 5.0 collective-permute-start.7
  84.3 3.5 collective-permute-start.8
  90.1 3.5 collective-permute-done.9
  101.1 12.5 %collective-permute-start.11 = (f32[4,18,34,1]{2,0,3,1:T(4,128)S(1)}, f32[4,18,34,1]{2,0,3,1:T(4,128)S(1)}, u32[]{:S(2)}, u32[]{:S(2)}) collective-permute-start(f32[4,18,34,1]{2,0,3,1:T(4,128)S(1)} %copy.104), channel_id=1, source_target_pairs={{1,0},{3,2},{5,4},{7,6},{9,8},{11,10},{13,12},{15,14},{17,16},{19,... | collective-permute-start | bytes 29384 | tf_op jit(solution)/shard_map/ppermute | solution.py:31
  117.3 3.4 pad_maximum_fusion.2
  123.8 43.7 %all-reduce = (f32[4]{0:T(128)S(1)}, f32[4]{0:T(128)S(1)}) all-reduce(f32[4]{0:T(128)S(1)} %get-tuple-element.4, f32[4]{0:T(128)S(1)} %get-tuple-element.3), channel_id=1, replica_groups=mesh['gx'=4,'gy'=4,'gz'=2] {'gx','gy','gz'}, use_global_device_ids=true, to_apply=%region_1.2 | all-reduce | flops 8 | bytes 64 | tf_op jit(solution)/shard_map/psum | solution.py:138
  167.4 2.9 fusion.42
  170.3 40.4 %psum.79 = f32[4]{0:T(128)S(1)} all-reduce(f32[4]{0:T(128)S(1)} %get-tuple-element.19), channel_id=1, replica_groups=mesh['gx'=4,'gy'=4,'gz'=2] {'gx','gy','gz'}, use_global_device_ids=true, to_apply=%region_5.6 | all-reduce | flops 4 | bytes 32 | tf_op jit(solution)/shard_map/psum | solution.py:138
  222.2 4.5 collective-permute-start.13
  228.7 2.5 collective-permute-start.14
  231.2 3.3 collective-permute-start.15
  234.6 2.5 collective-permute-done.15
  240.0 2.6 copy.113
  244.5 2.6 copy.114
  248.8 2.5 copy.115
  251.3 2.5 copy.116
  253.8 3.4 pad_maximum_fusion.3
  260.2 43.1 %psum.80 = f32[4]{0:T(128)S(1)} all-reduce(f32[4]{0:T(128)S(1)} %get-tuple-element.17), channel_id=1, replica_groups=mesh['gx'=4,'gy'=4,'gz'=2] {'gx','gy','gz'}, use_global_device_ids=true, to_apply=%region_7.8 | all-reduce | flops 4 | bytes 32 | tf_op jit(solution)/shard_map/psum | solution.py:146
  303.3 2.5 fusion.44
  305.8 40.2 %psum.81 = f32[4]{0:T(128)S(1)} all-reduce(f32[4]{0:T(128)S(1)} %get-tuple-element.15), channel_id=1, replica_groups=mesh['gx'=4,'gy'=4,'gz'=2] {'gx','gy','gz'}, use_global_device_ids=true, to_apply=%region_9.10 | all-reduce | flops 4 | bytes 32 | tf_op jit(solution)/shard_map/psum | solution.py:138
  357.4 4.5 collective-permute-start.19
  363.9 2.6 collective-permute-start.20
  366.5 3.3 collective-permute-start.21
  369.8 2.6 collective-permute-done.21
  384.9 3.7 pad_maximum_fusion.4
  391.3 42.3 %psum.82 = f32[4]{0:T(128)S(1)} all-reduce(f32[4]{0:T(128)S(1)} %get-tuple-element.13), channel_id=1, replica_groups=mesh['gx'=4,'gy'=4,'gz'=2] {'gx','gy','gz'}, use_global_device_ids=true, to_apply=%region_11.12 | all-reduce | flops 4 | bytes 32 | tf_op jit(solution)/shard_map/psum | solution.py:146
  433.6 2.8 fusion.46
  436.4 39.7 %psum.83 = f32[4]{0:T(128)S(1)} all-reduce(f32[4]{0:T(128)S(1)} %get-tuple-element.11), channel_id=1, replica_groups=mesh['gx'=4,'gy'=4,'gz'=2] {'gx','gy','gz'}, use_global_device_ids=true, to_apply=%region_13.14 | all-reduce | flops 4 | bytes 32 | tf_op jit(solution)/shard_map/psum | solution.py:138
  487.4 4.5 collective-permute-start.25
  493.9 3.3 collective-permute-start.26
  497.2 2.6 collective-permute-start.27
  499.8 3.3 collective-permute-done.27
  506.0 2.6 copy.133
  510.5 2.6 copy.134
  514.8 2.5 copy.135
  517.3 2.5 copy.136
  519.8 3.7 pad_maximum_fusion.5
  526.8 42.1 %psum.84 = f32[4]{0:T(128)S(1)} all-reduce(f32[4]{0:T(128)S(1)} %get-tuple-element.9), channel_id=1, replica_groups=mesh['gx'=4,'gy'=4,'gz'=2] {'gx','gy','gz'}, use_global_device_ids=true, to_apply=%region_15.16 | all-reduce | flops 4 | bytes 32 | tf_op jit(solution)/shard_map/psum | solution.py:146
  571.0 41.0 %psum.85 = f32[4]{0:T(128)S(1)} all-reduce(f32[4]{0:T(128)S(1)} %fusion.48), channel_id=1, replica_groups=mesh['gx'=4,'gy'=4,'gz'=2] {'gx','gy','gz'}, use_global_device_ids=true, to_apply=%region_17.18 | all-reduce | flops 4 | bytes 32 | tf_op jit(solution)/shard_map/psum | solution.py:138
  623.6 4.5 collective-permute-start.31
  630.1 2.6 collective-permute-start.32
  632.7 3.3 collective-permute-start.33
  636.0 2.5 collective-permute-done.33
  641.5 2.6 copy.143
  646.0 2.6 copy.144
  650.0 2.5 copy.145
  652.6 2.5 copy.146
  655.1 3.7 pad_maximum_fusion.6
  661.4 42.3 %psum.86 = f32[4]{0:T(128)S(1)} all-reduce(f32[4]{0:T(128)S(1)} %fusion.52), channel_id=1, replica_groups=mesh['gx'=4,'gy'=4,'gz'=2] {'gx','gy','gz'}, use_global_device_ids=true, to_apply=%region_19.20 | all-reduce | flops 4 | bytes 32 | tf_op jit(solution)/shard_map/psum | solution.py:146
  703.7 3.5 broadcast_multiply_fusion
  707.3 5.4 convolution_bitcast_fusion.25
  712.7 40.5 %psum.87 = f32[4,4]{1,0:T(4,128)S(1)} all-reduce(f32[4,4]{1,0:T(4,128)S(1)} %convolution_bitcast_fusion.25), channel_id=1, replica_groups=mesh['gx'=4,'gy'=4,'gz'=2] {'gx','gy','gz'}, use_global_device_ids=true, to_apply=%region_20.21 | all-reduce | flops 16 | bytes 128 | tf_op jit(solution)/shard_map/psum | solution.py:157
  762.1 2.4 fusion.72
  (354 shorter events, 156.6 us)
Async XLA Ops:
  5.2 64.7 %copy-start.37 = (f32[16,32,128]{2,1,0:T(8,128)}, f32[16,32,128]{2,1,0:T(8,128)S(1)}, u32[]{:S(2)}) copy-start(f32[16,32,128]{2,1,0:T(8,128)S(1)} %get-tuple-element.33) | copy-start | bytes 786436
  5.2 67.7 %copy-start.32 = (f32[16,32,128]{2,1,0:T(8,128)}, f32[16,32,128]{2,1,0:T(8,128)S(1)}, u32[]{:S(2)}) copy-start(f32[16,32,128]{2,1,0:T(8,128)S(1)} %get-tuple-element.34) | copy-start | bytes 786436
  5.2 348.2 %copy-start.9 = (f32[16,32,128]{2,1,0:T(8,128)}, f32[16,32,128]{2,1,0:T(8,128)S(1)}, u32[]{:S(2)}) copy-start(f32[16,32,128]{2,1,0:T(8,128)S(1)} %get-tuple-element.35) | copy-start | bytes 786436
  5.2 349.6 %copy-start.3 = (f32[16,32,128]{2,1,0:T(8,128)}, f32[16,32,128]{2,1,0:T(8,128)S(1)}, u32[]{:S(2)}) copy-start(f32[16,32,128]{2,1,0:T(8,128)S(1)} %get-tuple-element.37) | copy-start | bytes 786436
  5.3 349.6 %copy-start.6 = (f32[16,32,128]{2,1,0:T(8,128)}, f32[16,32,128]{2,1,0:T(8,128)S(1)}, u32[]{:S(2)}) copy-start(f32[16,32,128]{2,1,0:T(8,128)S(1)} %get-tuple-element.38) | copy-start | bytes 786436
  10.0 19.6 %copy-start.16 = (f32[11,16,32,128]{3,2,1,0:T(8,128)}, f32[11,16,32,128]{3,2,1,0:T(8,128)S(1)}, u32[]{:S(2)}) copy-start(f32[11,16,32,128]{3,2,1,0:T(8,128)S(1)} %constant_dynamic-update-slice_fusion) | copy-start | bytes 8650756
  10.0 9.0 %collective-permute-start = (f32[11,1,32,128]{3,2,1,0:T(8,128)S(1)}, f32[11,1,32,128]{3,2,1,0:T(8,128)S(1)}, u32[]{:S(2)}, u32[]{:S(2)}) collective-permute-start(f32[11,1,32,128]{3,2,1,0:T(8,128)S(1)} %get-tuple-element.30), channel_id=1, source_target_pairs={{0,8},{8,16},{16,24},{1,9},{9,17},{17,25},{2,10},{10,18},{18,26},{... | collective-permute-start | bytes 540680 | tf_op jit(solution)/shard_map/ppermute | solution.py:28
  11.3 8.1 %collective-permute-start.1 = (f32[11,1,32,128]{3,2,1,0:T(8,128)S(1)}, f32[11,1,32,128]{3,2,1,0:T(8,128)S(1)}, u32[]{:S(2)}, u32[]{:S(2)}) collective-permute-start(f32[11,1,32,128]{3,2,1,0:T(8,128)S(1)} %get-tuple-element.31), channel_id=1, source_target_pairs={{8,0},{16,8},{24,16},{9,1},{17,9},{25,17},{10,2},{18,10},{26,18},{... | collective-permute-start | bytes 540680 | tf_op jit(solution)/shard_map/ppermute | solution.py:31
  19.5 6.5 collective-permute-start.2
  23.0 6.5 collective-permute-start.3
  25.4 95.8 %copy-start.59 = (pred[32]{0:T(512)(128)(4,1)}, pred[32]{0:T(512)(128)(4,1)S(1)}, u32[]{:S(2)}) copy-start(pred[32]{0:T(512)(128)(4,1)S(1)} %get-tuple-element.82) | copy-start | bytes 100
  37.8 5.8 collective-permute-start.4
  42.3 4.4 collective-permute-start.5
  43.6 78.2 %copy-start.62 = (pred[128]{0:T(512)(128)(4,1)}, pred[128]{0:T(512)(128)(4,1)S(1)}, u32[]{:S(2)}) copy-start(pred[128]{0:T(512)(128)(4,1)S(1)} %get-tuple-element.83) | copy-start | bytes 388
  43.6 78.2 %copy-start.66 = (pred[128]{0:T(512)(128)(4,1)}, pred[128]{0:T(512)(128)(4,1)S(1)}, u32[]{:S(2)}) copy-start(pred[128]{0:T(512)(128)(4,1)S(1)} %get-tuple-element.84) | copy-start | bytes 388
  66.9 366.7 %copy-start.12 = (f32[16,32,128]{2,1,0:T(8,128)}, f32[16,32,128]{2,1,0:T(8,128)S(1)}, u32[]{:S(2)}) copy-start(f32[16,32,128]{2,1,0:T(8,128)S(1)} %get-tuple-element.29) | copy-start | bytes 786436
  75.6 6.9 collective-permute-start.6
  76.9 7.3 collective-permute-start.7
  84.3 5.9 collective-permute-start.8
  87.8 5.9 collective-permute-start.9
  97.9 15.8 %collective-permute-start.10 = (f32[4,18,34,1]{2,0,3,1:T(4,128)S(1)}, f32[4,18,34,1]{2,0,3,1:T(4,128)S(1)}, u32[]{:S(2)}, u32[]{:S(2)}) collective-permute-start(f32[4,18,34,1]{2,0,3,1:T(4,128)S(1)} %copy.103), channel_id=1, source_target_pairs={{0,1},{2,3},{4,5},{6,7},{8,9},{10,11},{12,13},{14,15},{16,17},{18,... | collective-permute-start | bytes 29384 | tf_op jit(solution)/shard_map/ppermute | solution.py:28
  101.1 14.3 %collective-permute-start.11 = (f32[4,18,34,1]{2,0,3,1:T(4,128)S(1)}, f32[4,18,34,1]{2,0,3,1:T(4,128)S(1)}, u32[]{:S(2)}, u32[]{:S(2)}) collective-permute-start(f32[4,18,34,1]{2,0,3,1:T(4,128)S(1)} %copy.104), channel_id=1, source_target_pairs={{1,0},{3,2},{5,4},{7,6},{9,8},{11,10},{13,12},{15,14},{17,16},{19,... | collective-permute-start | bytes 29384 | tf_op jit(solution)/shard_map/ppermute | solution.py:31
  170.3 43.0 %copy-start.42 = (f32[4,16,32,128]{3,2,1,0:T(8,128)}, f32[4,16,32,128]{3,2,1,0:T(8,128)S(1)}, u32[]{:S(2)}) copy-start(f32[4,16,32,128]{3,2,1,0:T(8,128)S(1)} %get-tuple-element.20) | copy-start | bytes 3145732
  220.9 6.2 collective-permute-start.12
  222.2 6.4 collective-permute-start.13
  228.6 8.4 %copy-start.50 = (f32[4,1,32,128]{3,2,1,0:T(8,128)}, f32[4,1,32,128]{3,2,1,0:T(8,128)S(1)}, u32[]{:S(2)}) copy-start(f32[4,1,32,128]{3,2,1,0:T(8,128)S(1)} %collective-permute-done.13) | copy-start | bytes 196612
  228.7 5.9 collective-permute-start.14
  231.2 5.9 collective-permute-start.15
  242.6 6.2 collective-permute-start.16
  247.1 4.2 collective-permute-start.17
  258.6 44.7 %copy-start.82 = (f32[4]{0:T(128)S(1)}, f32[4]{0:T(128)}, u32[]{:S(2)}) copy-start(f32[4]{0:T(128)} %copy-done.81) | copy-start | bytes 52
  258.6 44.7 %copy-start.43 = (f32[4,16,32,128]{3,2,1,0:T(8,128)S(1)}, f32[4,16,32,128]{3,2,1,0:T(8,128)}, u32[]{:S(2)}) copy-start(f32[4,16,32,128]{3,2,1,0:T(8,128)} %copy-done.42) | copy-start | bytes 3145732
  303.3 44.2 %copy-start.75 = (f32[4]{0:T(128)}, f32[4]{0:T(128)S(1)}, u32[]{:S(2)}) copy-start(f32[4]{0:T(128)S(1)} %div.43) | copy-start | bytes 52
  356.1 16.2 %copy-start.18 = (f32[4,16,32,128]{3,2,1,0:T(8,128)}, f32[4,16,32,128]{3,2,1,0:T(8,128)S(1)}, u32[]{:S(2)}) copy-start(f32[4,16,32,128]{3,2,1,0:T(8,128)S(1)} %fusion.28) | copy-start | bytes 3145732
  356.1 6.2 collective-permute-start.18
  357.4 6.4 collective-permute-start.19
  363.9 5.9 collective-permute-start.20
  366.5 5.9 collective-permute-start.21
  376.6 4.7 collective-permute-start.22
  379.9 3.3 collective-permute-start.23
  433.6 44.1 %copy-start.77 = (f32[4]{0:T(128)}, f32[4]{0:T(128)S(1)}, u32[]{:S(2)}) copy-start(f32[4]{0:T(128)S(1)} %div.45) | copy-start | bytes 52
  486.1 17.0 %copy-start.19 = (f32[4,16,32,128]{3,2,1,0:T(8,128)}, f32[4,16,32,128]{3,2,1,0:T(8,128)S(1)}, u32[]{:S(2)}) copy-start(f32[4,16,32,128]{3,2,1,0:T(8,128)S(1)} %fusion.27) | copy-start | bytes 3145732
  486.1 6.2 collective-permute-start.24
  487.4 6.4 collective-permute-start.25
  493.9 9.2 %copy-start.51 = (f32[4,1,32,128]{3,2,1,0:T(8,128)}, f32[4,1,32,128]{3,2,1,0:T(8,128)S(1)}, u32[]{:S(2)}) copy-start(f32[4,1,32,128]{3,2,1,0:T(8,128)S(1)} %collective-permute-done.25) | copy-start | bytes 196612
  493.9 5.9 collective-permute-start.26
  497.2 5.9 collective-permute-start.27
  508.6 6.2 collective-permute-start.28
  513.1 4.2 collective-permute-start.29
  525.2 43.7 %copy-start.84 = (f32[4]{0:T(128)S(1)}, f32[4]{0:T(128)}, u32[]{:S(2)}) copy-start(f32[4]{0:T(128)} %copy-done.83) | copy-start | bytes 52
  568.9 45.0 %copy-start.71 = (f32[4]{0:T(128)}, f32[4]{0:T(128)S(1)}, u32[]{:S(2)}) copy-start(f32[4]{0:T(128)S(1)} %div.47) | copy-start | bytes 52
  622.3 16.2 %copy-start.17 = (f32[4,16,32,128]{3,2,1,0:T(8,128)}, f32[4,16,32,128]{3,2,1,0:T(8,128)S(1)}, u32[]{:S(2)}) copy-start(f32[4,16,32,128]{3,2,1,0:T(8,128)S(1)} %fusion.26) | copy-start | bytes 3145732
  622.3 6.2 collective-permute-start.30
  623.6 6.4 collective-permute-start.31
  630.1 5.9 collective-permute-start.32
  632.7 5.9 collective-permute-start.33
  644.1 5.9 collective-permute-start.34
  648.6 4.0 collective-permute-start.35
  660.6 43.0 %copy-start.80 = (f32[4]{0:T(128)S(1)}, f32[4]{0:T(128)}, u32[]{:S(2)}) copy-start(f32[4]{0:T(128)} %copy-done.79) | copy-start | bytes 52
  660.6 43.0 %copy-start.72 = (f32[4]{0:T(128)S(1)}, f32[4]{0:T(128)}, u32[]{:S(2)}) copy-start(f32[4]{0:T(128)} %copy-done.71) | copy-start | bytes 52
  660.6 43.0 %copy-start.74 = (f32[4]{0:T(128)S(1)}, f32[4]{0:T(128)}, u32[]{:S(2)}) copy-start(f32[4]{0:T(128)} %copy-done.73) | copy-start | bytes 52
  660.6 43.0 %copy-start.76 = (f32[4]{0:T(128)S(1)}, f32[4]{0:T(128)}, u32[]{:S(2)}) copy-start(f32[4]{0:T(128)} %copy-done.75) | copy-start | bytes 52
  660.7 43.0 %copy-start.78 = (f32[4]{0:T(128)S(1)}, f32[4]{0:T(128)}, u32[]{:S(2)}) copy-start(f32[4]{0:T(128)} %copy-done.77) | copy-start | bytes 52
  707.2 49.1 %copy-start.26 = (f32[4,16,32,128]{3,2,1,0:T(8,128)S(1)}, f32[4,16,32,128]{3,2,1,0:T(8,128)}, u32[]{:S(2)}) copy-start(f32[4,16,32,128]{3,2,1,0:T(8,128)} %get-tuple-element.7) | copy-start | bytes 3145732
  (57 other events, 115.7 us)
where the time goes:
time: 772 us; the launch traced here: 765 us
  blocking collectives  415 us (54%)
  starting transfers between devices  100 us (13%)
  local copies, waits for them, and re-layouts  81 us (10%)
  other arithmetic  78.7 us (10%)
  matrix products  54.2 us (7%)
  waiting for transfers between devices  31.9 us (4%)
    psum x5, blocking collectives, residual_energy(): return lax.psum(products(residual, smooth), ('gx', 'gy', 'gz'))  205 us
    psum x4, blocking collectives, local(): alpha = energy / lax.psum(products(direction, image), ('gx', 'gy', 'gz'))  170 us
    ppermute x18, starting transfers between devices, padded_2(): lax.ppermute(lax.slice_in_dim(block, 0, width, axis=dim), axis, backward)  65 us
    psum x1, blocking collectives, local(): coupling = lax.psum(local_coupling, ('gx', 'gy', 'gz'))  40.5 us
    ppermute x18, starting transfers between devices, padded_2(): lax.ppermute(lax.slice_in_dim(block, block.shape[dim] - width, None, axis...  35.2 us
    concatenate x12, other arithmetic, padded_2(): block = jnp.concatenate([low, block, high], axis=dim)  30.1 us
    slice x18, local copies, waits for them, and re-layouts, padded_2(): lax.slice_in_dim(block, block.shape[dim] - width, None, axis=dim)  29.8 us
    ppermute x18, waiting for transfers between devices, padded_2(): lax.ppermute(lax.slice_in_dim(block, 0, width, axis=dim), axis, backward)  26.3 us
  transfers between devices with their start and end apart: 36, of which 19 were waited for; matrix products, arithmetic and copies ran while one was open for 4% of the time, Pallas kernels for 0%

commit v1 on v0

v1 whole, which is shorter than its diff:
```python
import functools

import jax
import jax.numpy as jnp
import numpy as np
from jax import lax
from jax.experimental import pallas as pl
from jax.experimental.pallas import tpu as pltpu
from jax.sharding import PartitionSpec as P

STEPS = 5
MESH = pl.DeviceIdType.MESH
F32 = jnp.float32
BF16 = jnp.bfloat16

gll_points = (
    -1.0,
    -0.8717401485096066,
    -0.5917001814331423,
    -0.2092992179024789,
    0.2092992179024789,
    0.5917001814331423,
    0.8717401485096066,
    1.0,
)


def gll_table():
    points = np.array(gll_points)
    values = (429.0 * points**7 - 693.0 * points**5 + 315.0 * points**3 - 35.0 * points) / 16.0
    table = np.zeros((8, 8))
    for row in range(8):
        for column in range(8):
            if row != column:
                table[row, column] = values[row] / (values[column] * (points[row] - points[column]))
    table[0, 0] = -14.0
    table[7, 7] = 14.0
    return table


TABLE = gll_table()


def halves(matrix):
    full = np.asarray(matrix, np.float32)
    high = full.astype(jnp.bfloat16)
    low = (full - high.astype(np.float32)).astype(jnp.bfloat16)
    return high, low


def left_matrices(height):
    eye = np.eye(height)
    squares = TABLE * TABLE
    return np.stack([np.stack(halves(np.kron(eye, m))) for m in (TABLE, TABLE.T, squares.T)])


def right_matrices(depth):
    eye = np.eye(depth // 8)
    squares = TABLE * TABLE
    out = []
    for m in (TABLE.T, TABLE, squares):
        high, low = halves(np.kron(eye, m))
        out.append(np.block([[high, low], [high, np.zeros_like(low)]]))
    return np.stack(out)


def mix_lines(matrix, lines):
    even = [lines[j] + lines[7 - j] for j in range(4)]
    odd = [lines[j] - lines[7 - j] for j in range(4)]
    out = [None] * 8
    for i in range(4):
        p = q = None
        for j in range(4):
            a = float(np.float32(0.5 * (matrix[i, j] + matrix[i, 7 - j])))
            b = float(np.float32(0.5 * (matrix[i, j] - matrix[i, 7 - j])))
            p = a * even[j] if p is None else p + a * even[j]
            q = b * odd[j] if q is None else q + b * odd[j]
        out[i] = q + p
        out[7 - i] = q - p
    return out


def split(v):
    high = v.astype(BF16)
    low = (v - high.astype(F32)).astype(BF16)
    return high, low


def dot(a, b):
    return jnp.dot(a, b, preferred_element_type=F32)


def left_apply(ly, kind, v):
    high, low = split(v)
    return (dot(ly[kind, 0], low) + dot(ly[kind, 1], high)) + dot(ly[kind, 0], high)


def right_apply(lz, kind, v):
    high, low = split(v)
    depth = v.shape[1]
    both = dot(jnp.concatenate([high, low], axis=1), lz[kind])
    return both[:, :depth] + both[:, depth:]


def fold8(v):
    total = v[0:8]
    for k in range(1, v.shape[0] // 8):
        total = total + v[8 * k : 8 * k + 8]
    return total


def kernel(
    dims, counts,
    metric, mass, shift, loads, inputs, ly, lz,
    rf, fb,
    lv, z, p, s, xs, r, wgt, pre, mtot, s2, s3, f2, f3, rr, acc, rows, state,
    zsend0, zrecv0, xsend0, xrecv0, ysend0, yrecv0, esend0, erecv0,
    zsend, zrecv, xsend, xrecv, ysend, yrecv, esend, erecv,
    asend, arecv,
    send0, recv0, send1, recv1, sendr, recvr,
):
    C, X, Y, Z = dims
    nx, ny, nz = counts
    N = nx * ny * nz
    E = X // 8
    R = 8 * Y
    XY = X * Y
    gx, gy, gz = lax.axis_index("gx"), lax.axis_index("gy"), lax.axis_index("gz")
    me = (gx * ny + gy) * nz + gz
    sh = shift[0]
    lane = lax.broadcasted_iota(jnp.int32, (8, Z), 1)

    def coords(number):
        rest = lax.div(number, nz)
        return (lax.div(rest, ny), lax.rem(rest, ny), lax.rem(number, nz))

    for ref in (zrecv0, xrecv0, yrecv0, erecv0, zrecv, xrecv, yrecv, erecv, esend0, esend):
        ref[...] = jnp.zeros(ref.shape, F32)

    barrier = pltpu.get_barrier_semaphore()

    def greet(i, carry):
        pl.semaphore_signal(
            barrier, inc=1, device_id=coords(lax.rem(me + i, N)), device_id_type=MESH
        )
        return carry

    lax.fori_loop(1, N, greet, 0)

    low_z = gz > 0
    high_z = gz < nz - 1
    low_of = {"x": gx > 0, "y": gy > 0}
    high_of = {"x": gx < nx - 1, "y": gy < ny - 1}
    inner0 = (lane % 8 == 0) & (lane > 0)
    inner7 = (lane % 8 == 7) & (lane < Z - 1)
    rim = (lane == 0) | (lane == Z - 1)

    def assemble(ncols, bufs, sems, par):
        zs, zr, xsn, xr, ysn, yr, es, er = bufs
        ssem, rsem = sems
        for c in range(ncols):
            for e in range(1, E):
                a = (c * X + 8 * e - 1) * Y
                t = lv[a : a + Y] + lv[a + Y : a + 2 * Y]
                lv[a : a + Y] = t
                lv[a + Y : a + 2 * Y] = t
        for k in range(1, Y // 8):
            first = pl.ds(8 * k - 1, ncols * X, stride=Y)
            second = pl.ds(8 * k, ncols * X, stride=Y)
            t = lv[first, :] + lv[second, :]
            lv[first, :] = t
            lv[second, :] = t

        def fold(c, carry):
            packed = jnp.zeros((8, Z), F32)
            for k in range(XY // 8):
                at = pl.ds(pl.multiple_of(c * XY + 8 * k, 8), 8)
                v = lv[at, :]
                v = v + jnp.where(
                    inner0, pltpu.roll(v, 1, 1), jnp.where(inner7, pltpu.roll(v, Z - 1, 1), 0.0)
                )
                lv[at, :] = v
                q = 2 * k
                moved = pltpu.roll(v, q, 1) if q else v
                packed = jnp.where((lane == q) | (lane == (q - 1) % Z), moved, packed)
            zs[pl.ds(pl.multiple_of(8 * c, 8), 8), :] = packed
            return carry

        lax.fori_loop(0, ncols, fold, 0)

        def zcopy(h):
            return pltpu.make_async_remote_copy(
                src_ref=zs,
                dst_ref=zr.at[par, 1 - h],
                send_sem=ssem.at[par, h],
                recv_sem=rsem.at[par, 1 - h],
                device_id=(gx, gy, gz + (2 * h - 1)),
                device_id_type=MESH,
            )

        zgoes = (low_z, high_z)
        for h in range(2):
            @pl.when(zgoes[h])
            def _():
                zcopy(h).start()
        for h in range(2):
            @pl.when(zgoes[1 - h])
            def _():
                zcopy(h).wait_recv()

        def unfold(c, carry):
            at = pl.ds(pl.multiple_of(8 * c, 8), 8)
            from_low = zr[par, 0, at, :]
            from_high = zr[par, 1, at, :]
            both = jnp.where(
                lane % 2 == 0, pltpu.roll(from_low, 1, 1), pltpu.roll(from_high, Z - 1, 1)
            )
            for k in range(XY // 8):
                at = pl.ds(pl.multiple_of(c * XY + 8 * k, 8), 8)
                q = (Z - 2 * k) % Z
                moved = pltpu.roll(both, q, 1) if q else both
                lv[at, :] = lv[at, :] + jnp.where(rim, moved, 0.0)
            return carry

        lax.fori_loop(0, ncols, unfold, 0)

        edge = (0, X - 1), (0, Y - 1)
        for h in range(2):
            for c in range(ncols):
                a = (c * X + edge[0][h]) * Y
                xsn[h, c * Y : (c + 1) * Y, :] = lv[a : a + Y]
            ysn[h] = lv[pl.ds(edge[1][h], ncols * X, stride=Y), :]
        for hx in range(2):
            for hy in range(2):
                for c in range(ncols):
                    a = (c * X + edge[0][hx]) * Y + edge[1][hy]
                    es[2 * hx + hy, c : c + 1, :] = lv[a : a + 1, :]

        plans = []
        for h in range(2):
            d = 2 * h - 1
            plans.append((
                (high_of if h else low_of)["x"], (low_of if h else high_of)["x"],
                xsn.at[h], xr.at[par, 1 - h], 2 + h, 2 + (1 - h), (gx + d, gy, gz),
            ))
            plans.append((
                (high_of if h else low_of)["y"], (low_of if h else high_of)["y"],
                ysn.at[h], yr.at[par, 1 - h], 4 + h, 4 + (1 - h), (gx, gy + d, gz),
            ))
        for hx in range(2):
            for hy in range(2):
                goes = (high_of if hx else low_of)["x"] & (high_of if hy else low_of)["y"]
                comes = (low_of if hx else high_of)["x"] & (low_of if hy else high_of)["y"]
                slot = 2 * (1 - hx) + (1 - hy)
                plans.append((
                    goes, comes, es.at[2 * hx + hy], er.at[par, slot],
                    6 + 2 * hx + hy, 6 + slot, (gx + 2 * hx - 1, gy + 2 * hy - 1, gz),
                ))

        def copy_of(plan):
            return pltpu.make_async_remote_copy(
                src_ref=plan[2],
                dst_ref=plan[3],
                send_sem=ssem.at[par, plan[4]],
                recv_sem=rsem.at[par, plan[5]],
                device_id=plan[6],
                device_id_type=MESH,
            )

        for plan in plans:
            @pl.when(plan[0])
            def _():
                copy_of(plan).start()
        for plan in plans:
            @pl.when(plan[1])
            def _():
                copy_of(plan).wait_recv()
        for h in range(2):
            for c in range(ncols):
                a = (c * X + edge[0][h]) * Y
                lv[a : a + Y] = lv[a : a + Y] + xr[par, h, c * Y : (c + 1) * Y, :]
            at = pl.ds(edge[1][h], ncols * X, stride=Y)
            lv[at, :] = lv[at, :] + yr[par, h]
        for hx in range(2):
            for hy in range(2):
                for c in range(ncols):
                    a = (c * X + edge[0][hx]) * Y + edge[1][hy]
                    lv[a : a + 1, :] = lv[a : a + 1, :] + er[par, 2 * hx + hy, c : c + 1, :]
        for h in range(2):
            @pl.when(zgoes[h])
            def _():
                zcopy(h).wait_send()
        for plan in plans:
            @pl.when(plan[0])
            def _():
                copy_of(plan).wait_send()

    squares = TABLE * TABLE
    row_of = lax.broadcasted_iota(jnp.int32, (Y, Z), 0)
    lane_of = lax.broadcasted_iota(jnp.int32, (Y, Z), 1)
    at_zero, at_seven = row_of % 8 == 0, row_of % 8 == 7
    ends_y = jnp.where(at_zero, -14.0, jnp.where(at_seven, 14.0, 0.0))
    ends_z = jnp.where(lane_of % 8 == 0, -14.0, jnp.where(lane_of % 8 == 7, 14.0, 0.0))
    wide = jnp.where(at_zero | at_seven, 0.5, 1.0)
    wide = jnp.where((row_of == 0) & (gy == 0), 1.0, wide)
    wide = jnp.where((row_of == Y - 1) & (gy == ny - 1), 1.0, wide)
    deep = jnp.where((lane_of % 8 == 0) | (lane_of % 8 == 7), 0.5, 1.0)
    deep = jnp.where((lane_of == 0) & (gz == 0), 1.0, deep)
    deep = jnp.where((lane_of == Z - 1) & (gz == nz - 1), 1.0, deep)
    plane = wide * deep
    for x in range(X):
        if x == 0:
            factor = jnp.where(gx > 0, 0.5, 1.0)
        elif x == X - 1:
            factor = jnp.where(gx < nx - 1, 0.5, 1.0)
        else:
            factor = 0.5 if x % 8 in (0, 7) else 1.0
        wgt[x * Y : (x + 1) * Y] = plane * factor

    lv[0 : C * XY] = loads[...]
    lv[(C + 1) * XY : (C + 2) * XY] = mass[...]
    for e in range(E):
        base = e * R
        rr[...] = left_apply(ly, 2, metric[1, base : base + R, :]) + right_apply(
            lz, 2, metric[2, base : base + R, :]
        )
        for i in range(8):
            a = base + i * Y
            total = rr[i * Y : (i + 1) * Y] + sh * mass[a : a + Y]
            for m in range(8):
                w = float(np.float32(squares[m, i]))
                if w != 0.0:
                    total = total + w * metric[0, base + m * Y : base + (m + 1) * Y, :]
            cross = ends_y * ends_z * metric[5, a : a + Y, :]
            if i in (0, 7):
                end = -14.0 if i == 0 else 14.0
                cross = cross + end * (
                    ends_y * metric[3, a : a + Y, :] + ends_z * metric[4, a : a + Y, :]
                )
            lv[C * XY + a : C * XY + a + Y] = total + 2.0 * cross
    zero = jnp.zeros((C * XY, Z), F32)
    p[...] = zero
    s[...] = zero
    xs[...] = zero
    rows[...] = jnp.zeros(rows.shape, F32)
    state[...] = jnp.zeros(state.shape, F32)

    pl.semaphore_wait(barrier, N - 1)
    assemble(
        C + 2,
        (zsend0, zrecv0, xsend0, xrecv0, ysend0, yrecv0, esend0, erecv0),
        (send0, recv0), 0,
    )
    rf[...] = lv[0 : C * XY]
    r[...] = lv[0 : C * XY]
    pre[...] = 1.0 / lv[C * XY : (C + 1) * XY]
    mtot[...] = lv[(C + 1) * XY : (C + 2) * XY]
    for c in range(C):
        z[c * XY : (c + 1) * XY] = pre[...] * lv[c * XY : (c + 1) * XY]

    def slab(i, carry):
        c = lax.div(i, E)
        e = i - c * E
        base = pl.multiple_of(i * R, R)
        ebase = pl.multiple_of(e * R, R)
        v = z[pl.ds(base, R), :]
        s2[...] = left_apply(ly, 0, v)
        s3[...] = right_apply(lz, 0, v)
        for t in range(Y // 8):
            va = [z[pl.ds(pl.multiple_of(base + a * Y + 8 * t, 8), 8), :] for a in range(8)]
            s1 = mix_lines(TABLE, va)
            f1 = []
            for m in range(8):
                o = m * Y + 8 * t
                at = pl.ds(pl.multiple_of(ebase + o, 8), 8)
                a, b, g = s1[m], s2[o : o + 8, :], s3[o : o + 8, :]
                m12, m13, m23 = metric[3, at, :], metric[4, at, :], metric[5, at, :]
                f1.append(metric[0, at, :] * a + m12 * b + m13 * g)
                f2[o : o + 8, :] = m12 * a + metric[1, at, :] * b + m23 * g
                f3[o : o + 8, :] = m13 * a + m23 * b + metric[2, at, :] * g
            r1 = mix_lines(TABLE.T, f1)
            for a in range(8):
                o = a * Y + 8 * t
                at = pl.ds(pl.multiple_of(ebase + o, 8), 8)
                rr[o : o + 8, :] = r1[a] + (sh * mass[at, :]) * va[a]
        out = rr[...] + left_apply(ly, 1, f2[...]) + right_apply(lz, 1, f3[...])
        lv[pl.ds(base, R), :] = out
        v = z[pl.ds(base, R), :]
        keep = jnp.where(e == 0, 0.0, 1.0)
        for j in range(C):
            term = fold8(v * inputs[pl.ds(pl.multiple_of(j * XY + ebase, R), R), :])
            acc[C * c + j] = keep * acc[C * c + j] + term
        term = fold8(wgt[pl.ds(ebase, R), :] * (r[pl.ds(base, R), :] * v))
        acc[C * C + c] = keep * acc[C * C + c] + term
        term = fold8(out * v)
        acc[C * C + C + c] = keep * acc[C * C + C + c] + term
        return carry

    def reduce_copy(i, par):
        peer = lax.rem(me + i, N)
        return pltpu.make_async_remote_copy(
            src_ref=asend,
            dst_ref=arecv.at[par, me],
            send_sem=sendr.at[i],
            recv_sem=recvr.at[par, me],
            device_id=coords(peer),
            device_id_type=MESH,
        )

    def arrive_copy(i, par):
        peer = lax.rem(me + i, N)
        return pltpu.make_async_remote_copy(
            src_ref=asend,
            dst_ref=arecv.at[par, peer],
            send_sem=sendr.at[i],
            recv_sem=recvr.at[par, peer],
            device_id=coords(peer),
            device_id_type=MESH,
        )

    def step(number, carry):
        par = lax.rem(number, 2)
        acc[...] = jnp.zeros(acc.shape, F32)
        lax.fori_loop(0, C * E, slab, 0)
        for c in range(C):
            for j in range(C):
                q = C * c + j
                rows[q : q + 1, :] = jnp.sum(acc[q], axis=0, keepdims=True)
            energy = jnp.sum(acc[C * C + c], axis=0, keepdims=True)
            curve = jnp.sum(acc[C * C + C + c], axis=0, keepdims=True)
            for j in range(C):
                q = C * c + j
                rows[C * C + q : C * C + q + 1, :] = energy
                rows[2 * C * C + q : 2 * C * C + q + 1, :] = curve
        part = jnp.sum(rows[...].T, axis=0, keepdims=True)
        asend[...] = part
        arecv[par, me] = part

        def push(i, carry):
            reduce_copy(i, par).start()
            return carry

        lax.fori_loop(1, N, push, 0)
        assemble(
            C,
            (zsend, zrecv, xsend, xrecv, ysend, yrecv, esend, erecv),
            (send1, recv1), par,
        )

        def gather(i, carry):
            arrive_copy(i, par).wait_recv()
            return carry

        lax.fori_loop(1, N, gather, 0)
        total = jnp.sum(arecv[par], axis=0)
        gamma = pltpu.roll(total, 128 - C * C, 1)
        delta = pltpu.roll(total, 128 - 2 * C * C, 1)
        used = lax.broadcasted_iota(jnp.int32, (1, 128), 1) < C * C
        gamma = jnp.where(used, gamma, 1.0)
        delta = jnp.where(used, delta, 1.0)
        fresh = number == 0
        old_gamma = jnp.where(fresh, 1.0, state[0:1, :])
        old_alpha = jnp.where(fresh, 1.0, state[1:2, :])
        beta = jnp.where(fresh, 0.0, gamma / old_gamma)
        alpha = gamma / (delta - beta * gamma / old_alpha)
        along = total + beta * state[2:3, :]
        state[0:1, :] = gamma
        state[1:2, :] = alpha
        state[2:3, :] = along
        state[3:4, :] = state[3:4, :] + alpha * along
        for c in range(C):
            b = jnp.broadcast_to(beta[:, C * c : C * c + 1], (Y, Z))
            a = jnp.broadcast_to(alpha[:, C * c : C * c + 1], (Y, Z))
            def update(x, carry):
                at = pl.ds(pl.multiple_of(c * XY + x * Y, Y), Y)
                pn = z[at, :] + b * p[at, :]
                sn = lv[at, :] + b * s[at, :]
                p[at, :] = pn
                s[at, :] = sn
                xs[at, :] = xs[at, :] + a * pn
                rn = r[at, :] - a * sn
                r[at, :] = rn
                z[at, :] = pre[pl.ds(pl.multiple_of(x * Y, Y), Y), :] * rn
                return carry
            lax.fori_loop(0, X, update, 0, unroll=4)

        def drain(i, carry):
            reduce_copy(i, par).wait_send()
            return carry

        lax.fori_loop(1, N, drain, 0)
        return carry

    lax.fori_loop(0, STEPS, step, 0)

    flat = state[3:4, :]
    k = [[flat[:, C * c + j : C * c + j + 1] for j in range(C)] for c in range(C)]
    y = [[None] * C for _ in range(C)]
    for a in range(C):
        for b in range(C):
            if b < a:
                y[a][b] = y[b][a]
                continue
            t = k[a][0] * k[b][0]
            for j in range(1, C):
                t = t + k[a][j] * k[b][j]
            y[a][b] = t + 1.0 if a == b else t
    one = jnp.ones((1, 1), F32)
    nil = jnp.zeros((1, 1), F32)
    right = [[one if a == b else nil for b in range(C)] + k[a] for a in range(C)]
    for a in range(C):
        inv = 1.0 / y[a][a]
        y[a] = [t * inv for t in y[a]]
        right[a] = [t * inv for t in right[a]]
        for b in range(C):
            if b != a:
                w = y[b][a]
                y[b] = [u - w * t for u, t in zip(y[b], y[a])]
                right[b] = [u - w * t for u, t in zip(right[b], right[a])]
    twice = 2.0 * sh
    coef = [[jnp.broadcast_to(twice * right[c][j], (8, Z)) for j in range(2 * C)] for c in range(C)]

    def finish(i, carry):
        at = pl.ds(pl.multiple_of(8 * i, 8), 8)
        m = mtot[at, :]
        heat = [m * xs[pl.ds(pl.multiple_of(c * XY + 8 * i, 8), 8), :] for c in range(C)]
        for j in range(C):
            at = pl.ds(pl.multiple_of(j * XY + 8 * i, 8), 8)
            t = heat[0] * coef[0][j]
            u = heat[0] * coef[0][C + j]
            for c in range(1, C):
                t = t + heat[c] * coef[c][j]
                u = u + heat[c] * coef[c][C + j]
            rf[at, :] = rf[at, :] - t
            fb[at, :] = u
        return carry

    lax.fori_loop(0, XY // 8, finish, 0, unroll=2)


def local(counts, metric, mass, shift, loads, inputs):
    C, X, Y, Z = loads.shape
    N = counts[0] * counts[1] * counts[2]
    XY = X * Y
    ly = jnp.asarray(left_matrices(Y))
    lz = jnp.asarray(right_matrices(Z))
    vm = lambda *shape: pltpu.VMEM(shape, F32)

    def comm(cols, pars):
        return [
            vm(8 * cols, Z), vm(pars, 2, 8 * cols, Z),
            vm(2, cols * Y, Z), vm(pars, 2, cols * Y, Z),
            vm(2, cols * X, Z), vm(pars, 2, cols * X, Z),
            vm(4, 8, Z), vm(pars, 4, 8, Z),
        ]

    dma = pltpu.SemaphoreType.DMA
    spec = pl.BlockSpec(memory_space=pltpu.VMEM)
    rf, fb = pl.pallas_call(
        functools.partial(kernel, (C, X, Y, Z), counts),
        out_shape=[jax.ShapeDtypeStruct((C * XY, Z), F32)] * 2,
        in_specs=[spec, spec, pl.BlockSpec(memory_space=pltpu.SMEM), spec, spec, spec, spec],
        out_specs=[spec, spec],
        scratch_shapes=[
            vm((C + 2) * XY, Z), vm(C * XY, Z), vm(C * XY, Z), vm(C * XY, Z), vm(C * XY, Z),
            vm(C * XY, Z), vm(XY, Z), vm(XY, Z), vm(XY, Z),
            vm(8 * Y, Z), vm(8 * Y, Z), vm(8 * Y, Z), vm(8 * Y, Z), vm(8 * Y, Z),
            vm(C * C + 2 * C, 8, Z), vm(128, Z), vm(8, 128),
        ]
        + comm(C + 2, 1)
        + comm(C, 2)
        + [vm(1, 128), vm(2, N, 1, 128)]
        + [dma((1, 10)), dma((1, 10)), dma((2, 10)), dma((2, 10)), dma((N,)), dma((2, N))],
        compiler_params=pltpu.CompilerParams(
            collective_id=0, has_side_effects=True, vmem_limit_bytes=56 << 20
        ),
    )(
        metric.reshape(6, XY, Z), mass.reshape(XY, Z), shift,
        loads.reshape(C * XY, Z), inputs.reshape(C * XY, Z), ly, lz,
    )
    return (rf.reshape(loads.shape), fb.reshape(loads.shape))


def solution(mesh):
    counts = tuple(mesh.shape[a] for a in ("gx", "gy", "gz"))
    return jax.shard_map(
        functools.partial(local, counts),
        mesh=mesh,
        in_specs=(
            P(None, "gx", "gy", "gz"),
            P("gx", "gy", "gz"),
            P(),
            P(None, "gx", "gy", "gz"),
            P(None, "gx", "gy", "gz"),
        ),
        out_specs=(P(None, "gx", "gy", "gz"), P(None, "gx", "gy", "gz")),
        check_vma=False,
    )
```

time: 772 us -> 133 us (0.17)
  blocking collectives: 415 us -> 0 us
  Pallas kernels: 0 us -> 128 us
  starting transfers between devices: 100 us -> 0 us
  other arithmetic: 78.7 us -> 0 us
  local copies, waits for them, and re-layouts: 81 us -> 3.32 us
  matrix products: 54.2 us -> 0 us
  waiting for transfers between devices: 31.9 us -> 0 us
    psum x10 -> x0, blocking collectives: 415 us -> none  [the longest x5 205 us: residual_energy(): return lax.psum(products(residual, smooth), ('gx', 'gy', 'gz'))]
    pallas_call x0 -> x1, Pallas kernels: none -> 128 us  [local(): pl.pallas_call(functools.partial(kernel, (C, X, Y, Z), counts), out_shape...]
    ppermute x36 -> x0, starting transfers between devices: 100 us -> none  [the longest x18 65 us: padded_2(): lax.ppermute(lax.slice_in_dim(block, 0, width, axis=dim), axis, backward)]
    dot_general x37 -> x0, matrix products: 53.4 us -> none  [the longest x11 16.6 us: derive_first(): jnp.einsum('ma,ceayz->cemyz', matrix, shaped, precision=lax.Precision.HIG...]
    slice x24 -> x0, local copies, waits for them, and re-layouts: 44.6 us -> none  [the longest x18 29.8 us: padded_2(): lax.slice_in_dim(block, block.shape[dim] - width, None, axis=dim)]
    ppermute x36 -> x0, waiting for transfers between devices: 31.9 us -> none  [the longest x18 26.3 us: padded_2(): lax.ppermute(lax.slice_in_dim(block, 0, width, axis=dim), axis, backward)]
    concatenate x12 -> x0, other arithmetic: 30.1 us -> none  [padded_2(): block = jnp.concatenate([low, block, high], axis=dim)]
    ppermute x12 -> x0, local copies, waits for them, and re-layouts: 28.5 us -> none  [the longest x6 14.2 us: padded_2(): lax.ppermute(lax.slice_in_dim(block, 0, width, axis=dim), axis, backward)]
  transfers between devices with their start and end apart: 36 -> 0, of which waited for: 19 -> 0; matrix products, arithmetic and copies ran while one was open for 4% -> 0% of each run, Pallas kernels for 0% -> 0%
where the time goes in v1:
time: 133 us; the launch traced here: 132 us
  Pallas kernels  128 us (96%)
  local copies, waits for them, and re-layouts  3.32 us (2%)
    pallas_call x1, Pallas kernels, local(): pl.pallas_call(functools.partial(kernel, (C, X, Y, Z), counts), out_shape...  128 us
    unnamed x4, local copies, waits for them, and re-layouts  3.32 us

profile of v1, /device:TPU:14, one launch (start us, length us, event | category | flops | bytes accessed | tf_op | source)
XLA Modules:
  0.0 132.2 jit_solution(14160532752340537415)
XLA Ops:
  1.3 127.6 %shard_map.86 = (f32[2048,128]{1,0:T(8,128)}, f32[2048,128]{1,0:T(8,128)}) custom-call(f32[6,512,128]{2,1,0:T(8,128)} %bitcast.6, f32[512,128]{1,0:T(8,128)} %bitcast.11, f32[1]{0:T(128)S(6)} %copy.11.shift, f32[2048,128]{1,0:T(8,128)} %bitcast.9, f32[2048,128]{1,0:T(8,128)} %bitcast.10, bf16[3,2,256,256]{3,2,1,0:T(8,128)(2,1)} %constant.4.clone.ly, ...), custom_call_target="tpu_custom_call" | custom-call | tf_op jit(solution)/shard_map/pallas_call | solution.py:559
  128.9 0.0 copy-start
  128.9 2.4 %copy.12 = f32[4,16,32,128]{3,2,1,0:T(8,128)} copy(f32[4,16,32,128]{3,2,1,0:T(8,128)} %bitcast.8) | data formatting | bytes 2097152
  131.2 0.0 copy-done
  131.2 1.0 copy.13
Async XLA Ops:
  128.9 2.4 %copy-start = (f32[2048,128]{1,0:T(8,128)S(1)}, f32[2048,128]{1,0:T(8,128)}, u32[]{:S(2)}) copy-start(f32[2048,128]{1,0:T(8,128)} %get-tuple-element.5) | copy-start | bytes 3145732

commit v2 on v1

--- a/solution.py
+++ b/solution.py
@@ -155,7 +155,7 @@
     inner7 = (lane % 8 == 7) & (lane < Z - 1)
     rim = (lane == 0) | (lane == Z - 1)
 
-    def assemble(ncols, bufs, sems, par):
+    def assemble(ncols, bufs, sems, par, meanwhile):
         zs, zr, xsn, xr, ysn, yr, es, er = bufs
         ssem, rsem = sems
         for c in range(ncols):
@@ -203,26 +203,34 @@
             @pl.when(zgoes[h])
             def _():
                 zcopy(h).start()
+        meanwhile()
         for h in range(2):
             @pl.when(zgoes[1 - h])
             def _():
                 zcopy(h).wait_recv()
 
-        def unfold(c, carry):
+        tiles = Y // 8
+        shown = [
+            k for k in range(XY // 8)
+            if k // tiles in (0, X - 1) or k % tiles in (0, tiles - 1)
+        ]
+        hidden = [k for k in range(XY // 8) if k not in shown]
+
+        def unfold(picked, c, carry):
             at = pl.ds(pl.multiple_of(8 * c, 8), 8)
             from_low = zr[par, 0, at, :]
             from_high = zr[par, 1, at, :]
             both = jnp.where(
                 lane % 2 == 0, pltpu.roll(from_low, 1, 1), pltpu.roll(from_high, Z - 1, 1)
             )
-            for k in range(XY // 8):
+            for k in picked:
                 at = pl.ds(pl.multiple_of(c * XY + 8 * k, 8), 8)
                 q = (Z - 2 * k) % Z
                 moved = pltpu.roll(both, q, 1) if q else both
                 lv[at, :] = lv[at, :] + jnp.where(rim, moved, 0.0)
             return carry
 
-        lax.fori_loop(0, ncols, unfold, 0)
+        lax.fori_loop(0, ncols, functools.partial(unfold, shown), 0)
 
         edge = (0, X - 1), (0, Y - 1)
         for h in range(2):
@@ -271,6 +279,8 @@
             @pl.when(plan[0])
             def _():
                 copy_of(plan).start()
+        if hidden:
+            lax.fori_loop(0, ncols, functools.partial(unfold, hidden), 0)
         for plan in plans:
             @pl.when(plan[1])
             def _():
@@ -338,10 +348,12 @@
                     ends_y * metric[3, a : a + Y, :] + ends_z * metric[4, a : a + Y, :]
                 )
             lv[C * XY + a : C * XY + a + Y] = total + 2.0 * cross
-    zero = jnp.zeros((C * XY, Z), F32)
-    p[...] = zero
-    s[...] = zero
-    xs[...] = zero
+    def clear():
+        zero = jnp.zeros((C * XY, Z), F32)
+        p[...] = zero
+        s[...] = zero
+        xs[...] = zero
+
     rows[...] = jnp.zeros(rows.shape, F32)
     state[...] = jnp.zeros(state.shape, F32)
 
@@ -349,7 +361,7 @@
     assemble(
         C + 2,
         (zsend0, zrecv0, xsend0, xrecv0, ysend0, yrecv0, esend0, erecv0),
-        (send0, recv0), 0,
+        (send0, recv0), 0, clear,
     )
     rf[...] = lv[0 : C * XY]
     r[...] = lv[0 : C * XY]
@@ -421,37 +433,36 @@
     def step(number, carry):
         par = lax.rem(number, 2)
         acc[...] = jnp.zeros(acc.shape, F32)
-        lax.fori_loop(0, C * E, slab, 0)
-        for c in range(C):
-            for j in range(C):
-                q = C * c + j
-                rows[q : q + 1, :] = jnp.sum(acc[q], axis=0, keepdims=True)
-            energy = jnp.sum(acc[C * C + c], axis=0, keepdims=True)
-            curve = jnp.sum(acc[C * C + C + c], axis=0, keepdims=True)
-            for j in range(C):
-                q = C * c + j
-                rows[C * C + q : C * C + q + 1, :] = energy
-                rows[2 * C * C + q : 2 * C * C + q + 1, :] = curve
-        part = jnp.sum(rows[...].T, axis=0, keepdims=True)
-        asend[...] = part
-        arecv[par, me] = part
-
-        def push(i, carry):
-            reduce_copy(i, par).start()
-            return carry
-
-        lax.fori_loop(1, N, push, 0)
+        lax.fori_loop(0, C * E, slab, 0, unroll=2)
+        def start_reduction():
+            for c in range(C):
+                for j in range(C):
+                    q = C * c + j
+                    rows[q : q + 1, :] = jnp.sum(acc[q], axis=0, keepdims=True)
+                energy = jnp.sum(acc[C * C + c], axis=0, keepdims=True)
+                curve = jnp.sum(acc[C * C + C + c], axis=0, keepdims=True)
+                for j in range(C):
+                    q = C * c + j
+                    rows[C * C + q : C * C + q + 1, :] = energy
+                    rows[2 * C * C + q : 2 * C * C + q + 1, :] = curve
+            part = jnp.sum(rows[...].T, axis=0, keepdims=True)
+            asend[...] = part
+            arecv[par, me] = part
+
+            def push(i, carry):
+                reduce_copy(i, par).start()
+                return carry
+
+            lax.fori_loop(1, N, push, 0)
+
         assemble(
             C,
             (zsend, zrecv, xsend, xrecv, ysend, yrecv, esend, erecv),
-            (send1, recv1), par,
+            (send1, recv1), par, start_reduction,
         )
 
-        def gather(i, carry):
+        for i in range(1, N):
             arrive_copy(i, par).wait_recv()
-            return carry
-
-        lax.fori_loop(1, N, gather, 0)
         total = jnp.sum(arecv[par], axis=0)
         gamma = pltpu.roll(total, 128 - C * C, 1)
         delta = pltpu.roll(total, 128 - 2 * C * C, 1)
@@ -484,17 +495,17 @@
                 return carry
             lax.fori_loop(0, X, update, 0, unroll=4)
 
-        def drain(i, carry):
+        for i in range(1, N):
             reduce_copy(i, par).wait_send()
-            return carry
-
-        lax.fori_loop(1, N, drain, 0)
         return carry
 
     lax.fori_loop(0, STEPS, step, 0)
 
     flat = state[3:4, :]
-    k = [[flat[:, C * c + j : C * c + j + 1] for j in range(C)] for c in range(C)]
+    k = [
+        [jnp.broadcast_to(flat[:, C * c + j : C * c + j + 1], (8, Z)) for j in range(C)]
+        for c in range(C)
+    ]
     y = [[None] * C for _ in range(C)]
     for a in range(C):
         for b in range(C):
@@ -505,8 +516,8 @@
             for j in range(1, C):
                 t = t + k[a][j] * k[b][j]
             y[a][b] = t + 1.0 if a == b else t
-    one = jnp.ones((1, 1), F32)
-    nil = jnp.zeros((1, 1), F32)
+    one = jnp.ones((8, Z), F32)
+    nil = jnp.zeros((8, Z), F32)
     right = [[one if a == b else nil for b in range(C)] + k[a] for a in range(C)]
     for a in range(C):
         inv = 1.0 / y[a][a]
@@ -518,7 +529,7 @@
                 y[b] = [u - w * t for u, t in zip(y[b], y[a])]
                 right[b] = [u - w * t for u, t in zip(right[b], right[a])]
     twice = 2.0 * sh
-    coef = [[jnp.broadcast_to(twice * right[c][j], (8, Z)) for j in range(2 * C)] for c in range(C)]
+    coef = [[twice * right[c][j] for j in range(2 * C)] for c in range(C)]
 
     def finish(i, carry):
         at = pl.ds(pl.multiple_of(8 * i, 8), 8)

time: 133 us -> 123 us (0.925)
  Pallas kernels: 128 us -> 118 us
    pallas_call x1, Pallas kernels: 128 us -> 118 us  [local(): pl.pallas_call(functools.partial(kernel, (C, X, Y, Z), counts), out_shape...]
where the time goes in v2:
time: 123 us; the launch traced here: 122 us
  Pallas kernels  118 us (96%)
  local copies, waits for them, and re-layouts  3.32 us (3%)
  between operations  1.29 us (1%)
    pallas_call x1, Pallas kernels, local(): pl.pallas_call(functools.partial(kernel, (C, X, Y, Z), counts), out_shape...  118 us
    unnamed x4, local copies, waits for them, and re-layouts  3.32 us

profile of v2, /device:TPU:14, one launch (start us, length us, event | category | flops | bytes accessed | tf_op | source)
XLA Modules:
  0.0 122.4 jit_solution(2999674328954722337)
XLA Ops:
  1.3 117.8 %shard_map.86 = (f32[2048,128]{1,0:T(8,128)}, f32[2048,128]{1,0:T(8,128)}) custom-call(f32[6,512,128]{2,1,0:T(8,128)} %bitcast.6, f32[512,128]{1,0:T(8,128)} %bitcast.11, f32[1]{0:T(128)S(6)} %copy.11.shift, f32[2048,128]{1,0:T(8,128)} %bitcast.9, f32[2048,128]{1,0:T(8,128)} %bitcast.10, bf16[3,2,256,256]{3,2,1,0:T(8,128)(2,1)} %constant.4.clone.ly, ...), custom_call_target="tpu_custom_call" | custom-call | tf_op jit(solution)/shard_map/pallas_call | solution.py:570
  119.1 0.0 copy-start
  119.1 2.4 %copy.12 = f32[4,16,32,128]{3,2,1,0:T(8,128)} copy(f32[4,16,32,128]{3,2,1,0:T(8,128)} %bitcast.8) | data formatting | bytes 2097152
  121.4 0.0 copy-done
  121.4 1.0 copy.13
Async XLA Ops:
  119.1 2.4 %copy-start = (f32[2048,128]{1,0:T(8,128)S(1)}, f32[2048,128]{1,0:T(8,128)}, u32[]{:S(2)}) copy-start(f32[2048,128]{1,0:T(8,128)} %get-tuple-element.5) | copy-start | bytes 3145732

commit v3 on v2

--- a/solution.py
+++ b/solution.py
@@ -186,7 +186,7 @@
             zs[pl.ds(pl.multiple_of(8 * c, 8), 8), :] = packed
             return carry
 
-        lax.fori_loop(0, ncols, fold, 0)
+        lax.fori_loop(0, ncols, fold, 0, unroll=2)
 
         def zcopy(h):
             return pltpu.make_async_remote_copy(
@@ -230,7 +230,7 @@
                 lv[at, :] = lv[at, :] + jnp.where(rim, moved, 0.0)
             return carry
 
-        lax.fori_loop(0, ncols, functools.partial(unfold, shown), 0)
+        lax.fori_loop(0, ncols, functools.partial(unfold, shown), 0, unroll=2)
 
         edge = (0, X - 1), (0, Y - 1)
         for h in range(2):
@@ -280,7 +280,7 @@
             def _():
                 copy_of(plan).start()
         if hidden:
-            lax.fori_loop(0, ncols, functools.partial(unfold, hidden), 0)
+            lax.fori_loop(0, ncols, functools.partial(unfold, hidden), 0, unroll=2)
         for plan in plans:
             @pl.when(plan[1])
             def _():
@@ -433,7 +433,7 @@
     def step(number, carry):
         par = lax.rem(number, 2)
         acc[...] = jnp.zeros(acc.shape, F32)
-        lax.fori_loop(0, C * E, slab, 0, unroll=2)
+        lax.fori_loop(0, C * E, slab, 0, unroll=4)
         def start_reduction():
             for c in range(C):
                 for j in range(C):
@@ -493,7 +493,7 @@
                 r[at, :] = rn
                 z[at, :] = pre[pl.ds(pl.multiple_of(x * Y, Y), Y), :] * rn
                 return carry
-            lax.fori_loop(0, X, update, 0, unroll=4)
+            lax.fori_loop(0, X, update, 0, unroll=8)
 
         for i in range(1, N):
             reduce_copy(i, par).wait_send()

time: 123 us -> 162 us (1.32)
  Pallas kernels: 118 us -> 157 us
    pallas_call x1, Pallas kernels: 118 us -> 157 us  [local(): pl.pallas_call(functools.partial(kernel, (C, X, Y, Z), counts), out_shape...]
where the time goes in v3:
time: 162 us; the launch traced here: 161 us
  Pallas kernels  157 us (97%)
  local copies, waits for them, and re-layouts  3.32 us (2%)
    pallas_call x1, Pallas kernels, local(): pl.pallas_call(functools.partial(kernel, (C, X, Y, Z), counts), out_shape...  157 us
    unnamed x4, local copies, waits for them, and re-layouts  3.32 us

profile of v3, /device:TPU:14, one launch (start us, length us, event | category | flops | bytes accessed | tf_op | source)
XLA Modules:
  0.0 161.5 jit_solution(15040584581627946798)
XLA Ops:
  1.3 156.8 %shard_map.86 = (f32[2048,128]{1,0:T(8,128)}, f32[2048,128]{1,0:T(8,128)}) custom-call(f32[6,512,128]{2,1,0:T(8,128)} %bitcast.6, f32[512,128]{1,0:T(8,128)} %bitcast.11, f32[1]{0:T(128)S(6)} %copy.11.shift, f32[2048,128]{1,0:T(8,128)} %bitcast.9, f32[2048,128]{1,0:T(8,128)} %bitcast.10, bf16[3,2,256,256]{3,2,1,0:T(8,128)(2,1)} %constant.4.clone.ly, ...), custom_call_target="tpu_custom_call" | custom-call | tf_op jit(solution)/shard_map/pallas_call | solution.py:570
  158.1 0.0 copy-start
  158.1 2.4 %copy.12 = f32[4,16,32,128]{3,2,1,0:T(8,128)} copy(f32[4,16,32,128]{3,2,1,0:T(8,128)} %bitcast.8) | data formatting | bytes 2097152
  160.5 0.0 copy-done
  160.5 1.0 copy.13
Async XLA Ops:
  158.1 2.4 %copy-start = (f32[2048,128]{1,0:T(8,128)S(1)}, f32[2048,128]{1,0:T(8,128)}, u32[]{:S(2)}) copy-start(f32[2048,128]{1,0:T(8,128)} %get-tuple-element.5) | copy-start | bytes 3145732
